TPU v7x, 32 devices: a whole 2x2x4 slice. The times are simulated.
32 devices in a mesh: sector: 8 (over y, x, core), term: 4 (over z).
Axes of the slice: x: 2, y: 2, z: 4, core: 2. Of those that a mesh axis runs over, the one named last changes fastest.
Arguments:
- x_start: float32 [8, 384, 384], P('sector', 'term'), may hold values from -6 to 6
- x_prev: float32 [8, 384, 384], P('sector', 'term'), may hold values from -6 to 6
- precond: float32 [8, 384, 384], P('sector', 'term'), may hold values from 0.5 to 6
- left_env: bfloat16 [256, 384, 384], P(('sector', 'term')), may hold values from -0.20412415 to 1.2041241
- right_env: bfloat16 [256, 384, 384], P(('sector', 'term')), may hold values from -0.20412415 to 1.2041241
- triples: int32 [640, 4], P(('sector', 'term')), may hold values from 0 to 63, as said below
- trip_count: int32 [8, 4], P('sector', 'term'), may hold values from 5 to 20, as said below
- term_coef: float32 [64], replicated, may hold values from 0.25 to 1
- lanczos_beta: float32 [3], replicated, may hold values from 0.3 to 1.2
- block_owner: int32 [8], replicated, may hold values from 0 to 7, each once
Outputs:
- final_vector: float32 [8, 384, 384], P('sector', 'term')
- rayleigh: float32 [3], replicated
Inputs may be any that keep to these rules, and one draw needn't show every extreme that they name: `triples`: Columns: a left slot below 8, a wavefunction block id below 8, a right slot below 8, an operator term below 64. `trip_count`: some device has exactly 20 live triples in every draw. `block_owner`: each sector index holds exactly one block.
All inputs are finite; a program needn't handle non-finite values.
Results may differ from a plain program's by a relative error of at most 0.006.
Values may be sent and summed in bfloat16 or wider, within the bound.
No kernel may reach another device: no remote copies, remote signals or barrier semaphores. Data moves between devices by JAX's collectives and lax.ppermute only.
A program may use at most 64 MiB of HBM per device.

v0:
```python
import math
import jax
import jax.numpy as jnp
from jax import lax
from jax.sharding import PartitionSpec as P

APPS = 3
EPSILON = 1e-06


def local(
    x_start,
    x_prev,
    precond,
    left_env,
    right_env,
    triples,
    trip_count,
    term_coef,
    lanczos_beta,
    block_owner,
):
    sectors = lax.axis_size("sector")
    term_count = lax.axis_size("term")
    block_size = left_env.shape[1]
    share_rows = x_start.shape[1]
    cell_count = sectors * block_size * block_size
    normaliser = 1.0 / math.sqrt(term_count * triples.shape[0])
    live_count = trip_count[0, 0]
    term_match = triples[:, 3:4] == jnp.arange(term_coef.shape[0], dtype=jnp.int32)[None, :]
    coefficient = jnp.sum(jnp.where(term_match, term_coef[None, :], 0.0), axis=1)
    owner_match = triples[:, 1:2] == jnp.arange(sectors, dtype=jnp.int32)[None, :]
    owner_rows = jnp.sum(jnp.where(owner_match, block_owner[None, :], 0), axis=1)

    def own_rows(array):
        return lax.dynamic_slice_in_dim(array, lax.axis_index("term") * share_rows, share_rows, 1)

    current, previous, diagonal = (
        lax.all_gather(x_start, "term", axis=1, tiled=True),
        lax.all_gather(x_prev, "term", axis=1, tiled=True),
        lax.all_gather(precond, "term", axis=1, tiled=True),
    )
    quotients = []
    for position in range(APPS):
        wave_half = current.astype(jnp.bfloat16)
        gathered = lax.all_gather(wave_half, "sector", axis=0, tiled=True)

        def add_triple(triple, accumulated):
            left_block = lax.dynamic_index_in_dim(left_env, triples[triple, 0], 0, keepdims=False)
            wave_block = lax.dynamic_index_in_dim(gathered, owner_rows[triple], 0, keepdims=False)
            right_block = lax.dynamic_index_in_dim(right_env, triples[triple, 2], 0, keepdims=False)
            middle = jnp.dot(left_block, wave_block, preferred_element_type=jnp.float32).astype(
                jnp.bfloat16
            )
            product = jnp.dot(middle, right_block, preferred_element_type=jnp.float32)
            return accumulated + coefficient[triple] * product

        start_sum = jnp.zeros((block_size, block_size), jnp.float32)
        applied = (lax.fori_loop(0, live_count, add_triple, start_sum) * normaliser)[None]
        applied = lax.psum(applied, "term")
        beta_now = lanczos_beta[position]
        cur_own = own_rows(current)
        app_own = own_rows(applied)
        prev_own = own_rows(previous)
        diag_own = own_rows(diagonal)
        diag_square = diag_own * diag_own
        weighted = diag_square * app_own
        weighted_cur = diag_square * cur_own
        sums_all = lax.psum(
            (
                jnp.sum(cur_own * app_own),
                jnp.sum(cur_own * cur_own),
                jnp.sum(weighted * app_own),
                jnp.sum(weighted * cur_own),
                jnp.sum(weighted * prev_own),
                jnp.sum(weighted_cur * cur_own),
                jnp.sum(weighted_cur * prev_own),
                jnp.sum(diag_square * prev_own * prev_own),
            ),
            ("sector", "term"),
        )
        (
            cross_sum,
            self_sum,
            image_image,
            image_current,
            image_previous,
            current_current,
            current_previous,
            previous_previous,
        ) = sums_all
        quotient = cross_sum / self_sum
        square_sum = (
            image_image
            - 2.0 * quotient * image_current
            - 2.0 * beta_now * image_previous
            + quotient * quotient * current_current
            + 2.0 * quotient * beta_now * current_previous
            + beta_now * beta_now * previous_previous
        )
        residual = applied - quotient * current - beta_now * previous
        scaled = diagonal * residual
        following = scaled / jnp.sqrt(square_sum / cell_count + EPSILON)
        previous, current = (current, following)
        quotients.append(quotient)
    return (own_rows(current), jnp.stack(quotients))


def solution(mesh):
    placed = (
        P("sector", "term", None),
        P("sector", "term", None),
        P("sector", "term", None),
        P(("sector", "term"), None, None),
        P(("sector", "term"), None, None),
        P(("sector", "term"), None),
        P("sector", "term"),
        P(),
        P(),
        P(),
    )
    return jax.shard_map(
        local,
        mesh=mesh,
        in_specs=placed,
        out_specs=(P("sector", "term", None), P()),
        check_vma=False,
    )
```

profile of v0, /device:TPU:0, one launch (start us, length us, event | category | flops | bytes accessed | tf_op | source)
XLA Modules:
  0.0 1039.4 jit_solution(10864611968168883217)
XLA Ops:
  7.2 18.5 %all_gather.19 = f32[1,384,384]{2,1,0:T(8,128)S(1)} all-gather(f32[1,96,384]{2,1,0:T(8,128)} %param.16), channel_id=1, replica_groups=mesh['sector'=8,'term'=4] {'term'}, dimensions={1}, use_global_device_ids=true | all-gather | bytes 737280 | tf_op jit(solution)/shard_map/all_gather | solution.py:39
  28.9 27.8 %all-gather.4.cloned.1.call-done = bf16[8,384,384]{2,1,0:T(8,128)(2,1)} async-done(((bf16[1,384,384]{2,1,0:T(8,128)(2,1)}), bf16[8,384,384]{2,1,0:T(8,128)(2,1)}) %all-gather.4.cloned.1.call-update) | async-done | bytes 2359312 | tf_op jit(solution)/shard_map/all_gather | solution.py:46
  56.8 105.1 %while.30 = (s32[]{:T(128)}, f32[384,384]{1,0:T(8,128)S(1)}, s32[]{:T(128)}, f32[20]{0:T(128)S(1)}, s32[20,4]{0,1:T(4,128)S(1)}, /*index=5*/bf16[8,384,384]{2,1,...) while((s32[]{:T(128)}, f32[384,384]{1,0:T(8,128)S(1)}, ...), condition=%wide.region_3.4_spmd, body=%wide.region_2.3_spmd.sunk | while | flops 226934800 | bytes 2065213 | solution.py:59
  165.4 33.6 %all_gather.18 = f32[1,384,384]{2,1,0:T(8,128)S(1)} all-gather(f32[1,96,384]{2,1,0:T(8,128)S(1)} %copy-done), channel_id=1, replica_groups=mesh['sector'=8,'term'=4] {'term'}, dimensions={1}, use_global_device_ids=true | all-gather | bytes 737280 | tf_op jit(solution)/shard_map/all_gather | solution.py:41
  199.0 16.4 %all_gather.21 = f32[1,384,384]{2,1,0:T(8,128)S(1)} all-gather(f32[1,96,384]{2,1,0:T(8,128)S(1)} %copy-done.1), channel_id=1, replica_groups=mesh['sector'=8,'term'=4] {'term'}, dimensions={1}, use_global_device_ids=true | all-gather | bytes 737280 | tf_op jit(solution)/shard_map/all_gather | solution.py:40
  215.4 97.2 %all-reduce.7.cloned.1.call-done = f32[1,384,384]{2,1,0:T(8,128)} async-done(((f32[1,384,384]{2,1,0:T(8,128)}), f32[1,384,384]{2,1,0:T(8,128)}) %all-reduce.7.cloned.1.call-update) | async-done | bytes 589840 | tf_op jit(solution)/shard_map/psum | solution.py:60
  314.3 42.7 %all-reduce.2 = (f32[]{:T(128)}, f32[]{:T(128)}, f32[]{:T(128)}, f32[]{:T(128)}, f32[]{:T(128)}, /*index=5*/f32[]{:T(128)}, f32[]{:T(128)}, f32[]{:T(128)}) all-reduce(f32[]{:T(128)} %get-tuple-element.167, f32[]{:T(128)} %get-tuple-element.166, f32[]{:T(128)} %get-tuple-element.168, ...), channel_id=1, replica_groups=mesh['sector'=8,'term'=4] {'sector','term'}, use_global_device_ids=true, to_apply=%region_10.11 | all-reduce | flops 8 | bytes 64 | tf_op jit(solution)/shard_map/psum | solution.py:69
  362.8 2.5 fusion.41
  365.4 29.6 %all-gather.6.cloned.1.call-done = bf16[8,384,384]{2,1,0:T(8,128)(2,1)} async-done(((bf16[1,384,384]{2,1,0:T(8,128)(2,1)}), bf16[8,384,384]{2,1,0:T(8,128)(2,1)}) %all-gather.6.cloned.1.call-update) | async-done | bytes 2359312 | tf_op jit(solution)/shard_map/all_gather | solution.py:46
  395.1 105.1 %while.31 = (s32[]{:T(128)}, f32[384,384]{1,0:T(8,128)S(1)}, s32[]{:T(128)}, f32[20]{0:T(128)S(1)}, s32[20,4]{0,1:T(4,128)S(1)}, /*index=5*/bf16[8,384,384]{2,1,...) while((s32[]{:T(128)}, f32[384,384]{1,0:T(8,128)S(1)}, ...), condition=%wide.region_22.23_spmd, body=%wide.region_21.22_spmd.sunk | while | flops 226934800 | bytes 2065213 | solution.py:59
  503.8 140.3 %all-reduce.9.cloned.1.call-done = f32[1,384,384]{2,1,0:T(8,128)} async-done(((f32[1,384,384]{2,1,0:T(8,128)}), f32[1,384,384]{2,1,0:T(8,128)}) %all-reduce.9.cloned.1.call-update) | async-done | bytes 589840 | tf_op jit(solution)/shard_map/psum | solution.py:60
  645.8 40.3 %all-reduce.1 = (f32[]{:T(128)}, f32[]{:T(128)}, f32[]{:T(128)}, f32[]{:T(128)}, f32[]{:T(128)}, /*index=5*/f32[]{:T(128)}, f32[]{:T(128)}) all-reduce(f32[]{:T(128)} %get-tuple-element.159, f32[]{:T(128)} %get-tuple-element.160, f32[]{:T(128)} %get-tuple-element.170, ...), channel_id=1, replica_groups=mesh['sector'=8,'term'=4] {'sector','term'}, use_global_device_ids=true, to_apply=%region_29.30 | all-reduce | flops 7 | bytes 56 | tf_op jit(solution)/shard_map/psum | solution.py:69
  691.3 2.6 fusion.40
  694.0 28.5 %all-gather.8.cloned.1.call-done = bf16[8,384,384]{2,1,0:T(8,128)(2,1)} async-done(((bf16[1,384,384]{2,1,0:T(8,128)(2,1)}), bf16[8,384,384]{2,1,0:T(8,128)(2,1)}) %all-gather.8.cloned.1.call-update) | async-done | bytes 2359312 | tf_op jit(solution)/shard_map/all_gather | solution.py:46
  722.5 110.6 %while.32 = (s32[]{:T(128)}, f32[384,384]{1,0:T(8,128)S(1)}, s32[]{:T(128)}, f32[20]{0:T(128)S(1)}, s32[20,4]{0,1:T(4,128)S(1)}, /*index=5*/bf16[8,384,384]{2,1,...) while((s32[]{:T(128)}, f32[384,384]{1,0:T(8,128)S(1)}, ...), condition=%wide.region_39.40_spmd, body=%wide.region_38.39_spmd.sunk | while | flops 226934800 | bytes 2065213 | solution.py:59
  731.0 2.5 fusion.66
  753.0 2.5 fusion.66
  764.0 2.5 fusion.66
  775.0 2.5 fusion.66
  786.0 2.5 fusion.66
  819.0 2.5 fusion.66
  830.0 2.5 fusion.66
  836.4 146.3 %all-reduce.11.cloned.1.call-done = f32[1,384,384]{2,1,0:T(8,128)} async-done(((f32[1,384,384]{2,1,0:T(8,128)}), f32[1,384,384]{2,1,0:T(8,128)}) %all-reduce.11.cloned.1.call-update) | async-done | bytes 589840 | tf_op jit(solution)/shard_map/psum | solution.py:60
  984.3 40.3 %all-reduce = (f32[]{:T(128)}, f32[]{:T(128)}, f32[]{:T(128)}, f32[]{:T(128)}, f32[]{:T(128)}, /*index=5*/f32[]{:T(128)}, f32[]{:T(128)}) all-reduce(f32[]{:T(128)} %get-tuple-element.152, f32[]{:T(128)} %get-tuple-element.153, f32[]{:T(128)} %get-tuple-element.169, ...), channel_id=1, replica_groups=mesh['sector'=8,'term'=4] {'sector','term'}, use_global_device_ids=true, to_apply=%region_46.47 | all-reduce | flops 7 | bytes 56 | tf_op jit(solution)/shard_map/psum | solution.py:69
  (149 shorter events, 126.1 us)
Async XLA Ops:
  7.2 49.6 %copy-start.2 = (s32[20,4]{0,1:T(4,128)S(1)}, s32[20,4]{0,1:T(4,128)}, u32[]{:S(2)}) copy-start(s32[20,4]{0,1:T(4,128)} %param.21) | copy-start | bytes 964
  7.2 49.5 %all-gather.4.cloned.1.call-start = ((), (), s32[]{:S(2)}) async-start(), calls=%async_computation | async-start | bytes 2654208 | tf_op jit(solution)/shard_map/all_gather | solution.py:46
  26.5 286.1 %all-reduce.7.cloned.1.call-start = ((), (), s32[]{:S(2)}) async-start(), calls=%async_computation.1 | async-start | bytes 1179648 | tf_op jit(solution)/shard_map/psum | solution.py:60
  56.8 106.1 %copy-start.3 = (f32[3]{0:T(128)S(1)}, f32[3]{0:T(128)}, u32[]{:S(2)}) copy-start(f32[3]{0:T(128)} %param.24) | copy-start | bytes 40
  56.8 108.6 %copy-start = (f32[1,96,384]{2,1,0:T(8,128)S(1)}, f32[1,96,384]{2,1,0:T(8,128)}, u32[]{:S(2)}) copy-start(f32[1,96,384]{2,1,0:T(8,128)} %param.18) | copy-start | bytes 442372
  161.9 37.1 %copy-start.1 = (f32[1,96,384]{2,1,0:T(8,128)S(1)}, f32[1,96,384]{2,1,0:T(8,128)}, u32[]{:S(2)}) copy-start(f32[1,96,384]{2,1,0:T(8,128)} %param.17) | copy-start | bytes 442372
  162.8 232.2 %all-gather.6.cloned.1.call-start = ((), (), s32[]{:S(2)}) async-start(), calls=%async_computation.2 | async-start | bytes 2654208 | tf_op jit(solution)/shard_map/all_gather | solution.py:46
  365.3 278.8 %all-reduce.9.cloned.1.call-start = ((), (), s32[]{:S(2)}) async-start(), calls=%async_computation.3 | async-start | bytes 1179648 | tf_op jit(solution)/shard_map/psum | solution.py:60
  501.0 221.4 %all-gather.8.cloned.1.call-start = ((), (), s32[]{:S(2)}) async-start(), calls=%async_computation.4 | async-start | bytes 2654208 | tf_op jit(solution)/shard_map/all_gather | solution.py:46
  693.9 288.7 %all-reduce.11.cloned.1.call-start = ((), (), s32[]{:S(2)}) async-start(), calls=%async_computation.5 | async-start | bytes 1179648 | tf_op jit(solution)/shard_map/psum | solution.py:60
Sparse Core Ops, SparseCore 0:
  26.6 30.0 all-gather.3
  162.9 149.6 all-reduce.6
  365.5 29.5 all-gather.5
  501.1 142.9 all-reduce.8
  694.0 28.3 all-gather.7
  834.1 148.4 all-reduce.10
where the time goes:
time: 1050 us; the launch traced here: 1040 us
  waiting for transfers between devices  470 us (45%)
  blocking collectives  192 us (18%)
  loops' own time  192 us (18%)
  matrix products  73.7 us (7%)
  local copies, waits for them, and re-layouts  56.9 us (5%)
  between operations  37.2 us (4%)
  other arithmetic  17.8 us (2%)
    psum x3, waiting for transfers between devices, local(): applied = lax.psum(applied, 'term')  384 us
    another operation x3, loops' own time, local(): lax.fori_loop(0, live_count, add_triple, start_sum) * normaliser  192 us
    psum x3, blocking collectives, local(): lax.psum((jnp.sum(cur_own * app_own), jnp.sum(cur_own * cur_own), jnp.sum...  123 us
    all_gather x3, waiting for transfers between devices, local(): gathered = lax.all_gather(wave_half, 'sector', axis=0, tiled=True)  86 us
    dot_general x30, matrix products, add_triple(): product = jnp.dot(middle, right_block, preferred_element_type=jnp.float32)  73.7 us
    all_gather x1, blocking collectives, local(): lax.all_gather(precond, 'term', axis=1, tiled=True)  33.6 us
  transfers between devices with their start and end apart: 6, of which 6 were waited for; matrix products, arithmetic and copies ran while one was open for 0% of the time, Pallas kernels for 0%

commit v1 on v0

--- a/solution.py
+++ b/solution.py
@@ -57,7 +57,8 @@
 
         start_sum = jnp.zeros((block_size, block_size), jnp.float32)
         applied = (lax.fori_loop(0, live_count, add_triple, start_sum) * normaliser)[None]
-        applied = lax.psum(applied, "term")
+        shards = lax.all_gather(applied, "term")
+        applied = jnp.sum(shards, axis=0)
         beta_now = lanczos_beta[position]
         cur_own = own_rows(current)
         app_own = own_rows(applied)

time: 1050 us -> 1060 us (level)
  waiting for transfers between devices: 470 us -> 492 us
    all_gather x0 -> x3, waiting for transfers between devices: none -> 405 us  [local(): shards = lax.all_gather(applied, 'term')]
    psum x3 -> x0, waiting for transfers between devices: 384 us -> none  [local(): applied = lax.psum(applied, 'term')]
where the time goes in v1:
time: 1060 us; the launch traced here: 1050 us
  waiting for transfers between devices  492 us (46%)
  blocking collectives  194 us (18%)
  loops' own time  185 us (17%)
  matrix products  72.2 us (7%)
  local copies, waits for them, and re-layouts  53.9 us (5%)
  between operations  36.5 us (3%)
  other arithmetic  17.7 us (2%)
    all_gather x3, waiting for transfers between devices, local(): shards = lax.all_gather(applied, 'term')  405 us
    another operation x3, loops' own time, local(): lax.fori_loop(0, live_count, add_triple, start_sum) * normaliser  185 us
    psum x3, blocking collectives, local(): lax.psum((jnp.sum(cur_own * app_own), jnp.sum(cur_own * cur_own), jnp.sum...  125 us
    all_gather x3, waiting for transfers between devices, local(): gathered = lax.all_gather(wave_half, 'sector', axis=0, tiled=True)  87 us
    dot_general x30, matrix products, add_triple(): product = jnp.dot(middle, right_block, preferred_element_type=jnp.float32)  72.2 us
    all_gather x1, blocking collectives, local(): lax.all_gather(precond, 'term', axis=1, tiled=True)  33.6 us
  transfers between devices with their start and end apart: 6, of which 6 were waited for; matrix products, arithmetic and copies ran while one was open for 0% of the time, Pallas kernels for 0%

profile of v1, /device:TPU:0, one launch (start us, length us, event | category | flops | bytes accessed | tf_op | source)
XLA Modules:
  0.0 1051.2 jit_solution(4836586084209074574)
XLA Ops:
  7.2 18.5 %all_gather.28 = f32[1,384,384]{2,1,0:T(8,128)S(1)} all-gather(f32[1,96,384]{2,1,0:T(8,128)} %param.16), channel_id=1, replica_groups=mesh['sector'=8,'term'=4] {'term'}, dimensions={1}, use_global_device_ids=true | all-gather | bytes 737280 | tf_op jit(solution)/shard_map/all_gather | solution.py:39
  28.9 27.8 %all-gather.10.cloned.1.call-done = bf16[8,384,384]{2,1,0:T(8,128)(2,1)} async-done(((bf16[1,384,384]{2,1,0:T(8,128)(2,1)}), bf16[8,384,384]{2,1,0:T(8,128)(2,1)}) %all-gather.10.cloned.1.call-update) | async-done | bytes 2359312 | tf_op jit(solution)/shard_map/all_gather | solution.py:46
  56.8 105.1 %while.30 = (s32[]{:T(128)}, f32[384,384]{1,0:T(8,128)S(1)}, s32[]{:T(128)}, f32[20]{0:T(128)S(1)}, s32[20,4]{0,1:T(4,128)S(1)}, /*index=5*/bf16[8,384,384]{2,1,...) while((s32[]{:T(128)}, f32[384,384]{1,0:T(8,128)S(1)}, ...), condition=%wide.region_3.4_spmd, body=%wide.region_2.3_spmd.sunk | while | flops 226934800 | bytes 2065213 | solution.py:59
  64.8 2.4 fusion.75
  165.3 33.6 %all_gather.27 = f32[1,384,384]{2,1,0:T(8,128)S(1)} all-gather(f32[1,96,384]{2,1,0:T(8,128)S(1)} %copy-done), channel_id=1, replica_groups=mesh['sector'=8,'term'=4] {'term'}, dimensions={1}, use_global_device_ids=true | all-gather | bytes 737280 | tf_op jit(solution)/shard_map/all_gather | solution.py:41
  198.9 16.4 %all_gather.31 = f32[1,384,384]{2,1,0:T(8,128)S(1)} all-gather(f32[1,96,384]{2,1,0:T(8,128)S(1)} %copy-done.1), channel_id=1, replica_groups=mesh['sector'=8,'term'=4] {'term'}, dimensions={1}, use_global_device_ids=true | all-gather | bytes 737280 | tf_op jit(solution)/shard_map/all_gather | solution.py:40
  215.3 108.0 %all-gather.16.cloned.1.call-done = f32[1536,384]{1,0:T(8,128)} async-done(((f32[384,384]{1,0:T(8,128)}), f32[1536,384]{1,0:T(8,128)}) %all-gather.16.cloned.1.call-update) | async-done | bytes 2359312 | tf_op jit(solution)/shard_map/all_gather | solution.py:60
  326.0 46.6 %all-reduce.2 = (f32[]{:T(128)}, f32[]{:T(128)}, f32[]{:T(128)}, f32[]{:T(128)}, f32[]{:T(128)}, /*index=5*/f32[]{:T(128)}, f32[]{:T(128)}, f32[]{:T(128)}) all-reduce(f32[]{:T(128)} %get-tuple-element.167, f32[]{:T(128)} %get-tuple-element.166, f32[]{:T(128)} %get-tuple-element.168, ...), channel_id=1, replica_groups=mesh['sector'=8,'term'=4] {'sector','term'}, use_global_device_ids=true, to_apply=%region_10.11 | all-reduce | flops 8 | bytes 64 | tf_op jit(solution)/shard_map/psum | solution.py:70
  379.9 30.2 %all-gather.12.cloned.1.call-done = bf16[8,384,384]{2,1,0:T(8,128)(2,1)} async-done(((bf16[1,384,384]{2,1,0:T(8,128)(2,1)}), bf16[8,384,384]{2,1,0:T(8,128)(2,1)}) %all-gather.12.cloned.1.call-update) | async-done | bytes 2359312 | tf_op jit(solution)/shard_map/all_gather | solution.py:46
  410.2 107.1 %while.31 = (s32[]{:T(128)}, f32[384,384]{1,0:T(8,128)S(1)}, s32[]{:T(128)}, f32[20]{0:T(128)S(1)}, s32[20,4]{0,1:T(4,128)S(1)}, /*index=5*/bf16[8,384,384]{2,1,...) while((s32[]{:T(128)}, f32[384,384]{1,0:T(8,128)S(1)}, ...), condition=%wide.region_22.23_spmd, body=%wide.region_21.22_spmd.sunk | while | flops 226934800 | bytes 2065213 | solution.py:59
  418.4 2.4 fusion.79
  429.1 2.4 fusion.79
  439.7 2.4 fusion.79
  450.4 2.4 fusion.79
  461.0 2.4 fusion.79
  471.6 2.4 fusion.79
  482.3 2.4 fusion.79
  492.9 2.4 fusion.79
  520.5 153.1 %all-gather.18.cloned.1.call-done = f32[1536,384]{1,0:T(8,128)} async-done(((f32[384,384]{1,0:T(8,128)}), f32[1536,384]{1,0:T(8,128)}) %all-gather.18.cloned.1.call-update) | async-done | bytes 2359312 | tf_op jit(solution)/shard_map/all_gather | solution.py:60
  676.3 39.4 %all-reduce.1 = (f32[]{:T(128)}, f32[]{:T(128)}, f32[]{:T(128)}, f32[]{:T(128)}, f32[]{:T(128)}, /*index=5*/f32[]{:T(128)}, f32[]{:T(128)}) all-reduce(f32[]{:T(128)} %get-tuple-element.159, f32[]{:T(128)} %get-tuple-element.160, f32[]{:T(128)} %get-tuple-element.170, ...), channel_id=1, replica_groups=mesh['sector'=8,'term'=4] {'sector','term'}, use_global_device_ids=true, to_apply=%region_29.30 | all-reduce | flops 7 | bytes 56 | tf_op jit(solution)/shard_map/psum | solution.py:70
  722.3 29.0 %all-gather.14.cloned.1.call-done = bf16[8,384,384]{2,1,0:T(8,128)(2,1)} async-done(((bf16[1,384,384]{2,1,0:T(8,128)(2,1)}), bf16[8,384,384]{2,1,0:T(8,128)(2,1)}) %all-gather.14.cloned.1.call-update) | async-done | bytes 2359312 | tf_op jit(solution)/shard_map/all_gather | solution.py:46
  751.3 97.4 %while.32 = (s32[]{:T(128)}, f32[384,384]{1,0:T(8,128)S(1)}, s32[]{:T(128)}, f32[20]{0:T(128)S(1)}, s32[20,4]{0,1:T(4,128)S(1)}, /*index=5*/bf16[8,384,384]{2,1,...) while((s32[]{:T(128)}, f32[384,384]{1,0:T(8,128)S(1)}, ...), condition=%wide.region_39.40_spmd, body=%wide.region_38.39_spmd.sunk | while | flops 226934800 | bytes 2065213 | solution.py:59
  852.0 143.5 %all-gather.20.cloned.1.call-done = f32[1536,384]{1,0:T(8,128)} async-done(((f32[384,384]{1,0:T(8,128)}), f32[1536,384]{1,0:T(8,128)}) %all-gather.20.cloned.1.call-update) | async-done | bytes 2359312 | tf_op jit(solution)/shard_map/all_gather | solution.py:60
  998.1 39.4 %all-reduce = (f32[]{:T(128)}, f32[]{:T(128)}, f32[]{:T(128)}, f32[]{:T(128)}, f32[]{:T(128)}, /*index=5*/f32[]{:T(128)}, f32[]{:T(128)}) all-reduce(f32[]{:T(128)} %get-tuple-element.152, f32[]{:T(128)} %get-tuple-element.153, f32[]{:T(128)} %get-tuple-element.169, ...), channel_id=1, replica_groups=mesh['sector'=8,'term'=4] {'sector','term'}, use_global_device_ids=true, to_apply=%region_46.47 | all-reduce | flops 7 | bytes 56 | tf_op jit(solution)/shard_map/psum | solution.py:70
  (152 shorter events, 122.2 us)
Async XLA Ops:
  7.2 49.6 %copy-start.2 = (s32[20,4]{0,1:T(4,128)S(1)}, s32[20,4]{0,1:T(4,128)}, u32[]{:S(2)}) copy-start(s32[20,4]{0,1:T(4,128)} %param.21) | copy-start | bytes 964
  7.2 49.5 %all-gather.10.cloned.1.call-start = ((), (), s32[]{:S(2)}) async-start(), calls=%async_computation | async-start | bytes 2654208 | tf_op jit(solution)/shard_map/all_gather | solution.py:46
  26.5 296.9 %all-gather.16.cloned.1.call-start = ((), (), s32[]{:S(2)}) async-start(), calls=%async_computation.3 | async-start | bytes 2949120 | tf_op jit(solution)/shard_map/all_gather | solution.py:60
  56.8 106.1 %copy-start.3 = (f32[3]{0:T(128)S(1)}, f32[3]{0:T(128)}, u32[]{:S(2)}) copy-start(f32[3]{0:T(128)} %param.24) | copy-start | bytes 40
  56.8 108.6 %copy-start = (f32[1,96,384]{2,1,0:T(8,128)S(1)}, f32[1,96,384]{2,1,0:T(8,128)}, u32[]{:S(2)}) copy-start(f32[1,96,384]{2,1,0:T(8,128)} %param.18) | copy-start | bytes 442372
  161.9 37.0 %copy-start.1 = (f32[1,96,384]{2,1,0:T(8,128)S(1)}, f32[1,96,384]{2,1,0:T(8,128)}, u32[]{:S(2)}) copy-start(f32[1,96,384]{2,1,0:T(8,128)} %param.17) | copy-start | bytes 442372
  162.8 247.4 %all-gather.12.cloned.1.call-start = ((), (), s32[]{:S(2)}) async-start(), calls=%async_computation.1 | async-start | bytes 2654208 | tf_op jit(solution)/shard_map/all_gather | solution.py:46
  379.9 293.8 %all-gather.18.cloned.1.call-start = ((), (), s32[]{:S(2)}) async-start(), calls=%async_computation.4 | async-start | bytes 2949120 | tf_op jit(solution)/shard_map/all_gather | solution.py:60
  518.2 233.0 %all-gather.14.cloned.1.call-start = ((), (), s32[]{:S(2)}) async-start(), calls=%async_computation.2 | async-start | bytes 2654208 | tf_op jit(solution)/shard_map/all_gather | solution.py:46
  722.2 273.2 %all-gather.20.cloned.1.call-start = ((), (), s32[]{:S(2)}) async-start(), calls=%async_computation.5 | async-start | bytes 2949120 | tf_op jit(solution)/shard_map/all_gather | solution.py:60
Sparse Core Ops, SparseCore 0:
  26.6 30.0 all-gather.9
  162.9 160.3 all-gather.15
  380.0 30.1 all-gather.11
  518.3 155.2 all-gather.17
  722.4 28.8 all-gather.13
  849.8 145.6 all-gather.19
